TPU v7x, 32 devices: a whole 2x2x4 slice. The times are simulated.
32 devices in a mesh: fsdp: 8 (over y, x, core), ep: 4 (over z).
Axes of the slice: x: 2, y: 2, z: 4, core: 2. Of those that a mesh axis runs over, the one named last changes fastest.
Arguments:
- hidden: bfloat16 [2048, 8192], P('fsdp', 'ep'), may hold values from -6 to 6
- w_down: bfloat16 [6144, 2, 8192], P('fsdp', None, 'ep'), may hold values from -0.0625 to 0.0625
- route_ids: int32 [1024, 2], P('fsdp'), may hold values from 0 to 7, as said below
- probs: float32 [1024, 2], P('fsdp'), may hold values from 0.1 to 0.9
- grad_out: bfloat16 [1024, 6144], P('fsdp', 'ep'), may hold values from -6 to 6
Outputs:
- output: bfloat16 [1024, 6144], P('fsdp', 'ep')
- grad_hidden: bfloat16 [2048, 8192], P('fsdp', 'ep')
- grad_weight: bfloat16 [6144, 2, 8192], P('fsdp', None, 'ep')
- grad_probs: float32 [1024, 2], P('fsdp')
Inputs may be any that keep to these rules, and one draw needn't show every extreme that they name: `route_ids`: each token names 2 different experts. Within one panel's 128 tokens, experts 0 and 1 are each named by 1 to 128 tokens, and in some panel both are named by all 128 tokens.
All inputs are finite; a program needn't handle non-finite values.
Results may differ from a plain program's by a relative error of at most 0.012.
Values may be sent and summed in bfloat16 or wider, within the bound.
A program may use at most 384 MiB of HBM per device.

v0:
```python
import jax
import jax.numpy as jnp
from jax import lax
from jax.sharding import PartitionSpec as P

BLOCK = 128


def route_layout(route_part, prob_part, expert_count, block_rows, row_count):
    token_count = route_part.shape[0]
    experts = jnp.arange(expert_count, dtype=jnp.int32)
    hits = (route_part[:, :, None] == experts[None, None, :]).astype(jnp.int32)
    named = jnp.sum(hits, axis=1)
    counts = jnp.sum(named, axis=0)
    ranks = jnp.cumsum(named, axis=0) - named
    padded = (counts + block_rows - 1) // block_rows * block_rows
    offsets = jnp.cumsum(padded) - padded
    row_of = jnp.sum(hits * (offsets[None, None, :] + ranks[:, None, :]), axis=2)
    valid = jnp.sum(hits, axis=2)
    starts = jnp.arange(row_count // block_rows, dtype=jnp.int32) * block_rows
    inside = (starts[:, None] >= offsets[None, :]) & (starts[:, None] < (offsets + padded)[None, :])
    block_exp = jnp.sum(jnp.where(inside, experts[None, :] + 1, 0), axis=1) - 1
    target = jnp.where(valid > 0, row_of, row_count).reshape(-1)
    token_index = jnp.broadcast_to(
        jnp.arange(token_count, dtype=jnp.int32)[:, None], route_part.shape
    ).reshape(-1)
    row_tok = jnp.zeros((row_count,), jnp.int32).at[target].set(token_index, mode="drop")
    row_live = (
        jnp.zeros((row_count,), jnp.int32).at[target].set(jnp.ones_like(token_index), mode="drop")
    )
    row_prob = (
        jnp.zeros((row_count,), prob_part.dtype).at[target].set(prob_part.reshape(-1), mode="drop")
    )
    return (row_of, valid, block_exp, row_tok, row_live, row_prob)


def local(hidden, w_down, route_ids, probs, grad_out):
    row_count, unit_count = hidden.shape
    expert_count = w_down.shape[1]
    block_count = row_count // BLOCK
    row_of, valid, block_exp, row_tok, row_live, row_prob = route_layout(
        route_ids, probs, expert_count, BLOCK, row_count
    )
    safe_exp = jnp.maximum(block_exp, 0)
    prob_valid = probs * valid.astype(jnp.float32)
    full_grads = lax.all_gather(grad_out, "ep", axis=1, tiled=True)
    model_width = full_grads.shape[1]
    routed = jnp.where(row_live[:, None] > 0, full_grads[row_tok], jnp.zeros((), jnp.bfloat16))
    scaled = (row_prob[:, None] * routed.astype(jnp.float32)).astype(jnp.bfloat16)
    hid_blocks = hidden.reshape(block_count, BLOCK, unit_count)
    routed_blocks = routed.reshape(block_count, BLOCK, model_width)
    row_exp = jnp.repeat(block_exp, BLOCK)
    member = (row_exp[:, None] == jnp.arange(expert_count, dtype=jnp.int32)[None, :]).astype(
        jnp.bfloat16
    )
    masked_hid = hidden[:, None, :] * member[:, :, None]
    piece = lax.all_gather(w_down, "fsdp", axis=0, tiled=True)
    width = piece.shape[0]
    chosen = jnp.take(piece, safe_exp, axis=1)
    out_rows = jnp.einsum(
        "bri,dbi->brd", hid_blocks, chosen, preferred_element_type=jnp.float32
    ).reshape(row_count, width)
    back_total = jnp.einsum(
        "brd,dbi->bri", routed_blocks, chosen, preferred_element_type=jnp.float32
    )
    combined = jnp.sum(prob_valid[:, :, None] * out_rows[row_of], axis=1)
    out_total = combined
    out_total, back_total = (out_total, back_total)
    grad_weight = lax.psum_scatter(
        jnp.einsum("rd,rei->dei", scaled, masked_hid, preferred_element_type=jnp.float32).astype(
            jnp.bfloat16
        ),
        "fsdp",
        scatter_dimension=0,
        tiled=True,
    )
    output = lax.psum_scatter(out_total.astype(jnp.bfloat16), "ep", scatter_dimension=1, tiled=True)
    hidden_back = back_total.reshape(row_count, unit_count)
    grad_hidden = (row_prob[:, None] * hidden_back).astype(jnp.bfloat16)
    row_dot = jnp.sum(hidden.astype(jnp.float32) * hidden_back, axis=1)
    prob_terms = valid.astype(jnp.float32) * row_dot[row_of]
    grad_probs = lax.psum(prob_terms, "ep")
    return (output, grad_hidden, grad_weight, grad_probs)


def solution(mesh):
    placed = (
        P("fsdp", "ep"),
        P("fsdp", None, "ep"),
        P("fsdp", None),
        P("fsdp", None),
        P("fsdp", "ep"),
    )
    return jax.shard_map(
        local,
        mesh=mesh,
        in_specs=placed,
        out_specs=(P("fsdp", "ep"), P("fsdp", "ep"), P("fsdp", None, "ep"), P("fsdp", None)),
        check_vma=False,
    )
```

profile of v0, /device:TPU:0, one launch (start us, length us, event | category | flops | bytes accessed | tf_op | source)
XLA Modules:
  0.0 635.5 jit_solution(14992355778642910269)
XLA Ops:
  23.5 25.9 %all-gather.5.cloned.1.call-done = bf16[128,6144]{1,0:T(8,128)(2,1)} async-done(((bf16[128,1536]{1,0:T(8,128)(2,1)}), bf16[128,6144]{1,0:T(8,128)(2,1)}) %all-gather.5.cloned.1.call-update) | async-done | bytes 1572880 | tf_op jit(solution)/shard_map/all_gather | solution.py:46
  56.5 24.9 %convolution_convert_fusion = bf16[6144,2,2048]{2,0,1:T(8,128)(2,1)} fusion(bf16[256,6144]{1,0:T(8,128)(2,1)S(1)} %gather_fusion.1, f32[256]{0:T(256)S(1)} %scatter_custom_fusion, pred[256]{0:T(512)(128)(4,1)S(1)} %broadcast_compare_fusion, bf16[256,2]{0,1:T(2,128)(2,1)S(1)} %compare_convert_fusion, bf16[256,2048]{1,0:T(8,128)(2,1)} %param.5), kind=kOutput, calls=%fused_computation.31 | convolution fusion | flops 12920553472 | bytes 54528256 | tf_op jit(solution)/shard_map/rd,rei->dei/dot_general | solution.py:70
  83.2 199.5 %all-gather.3.cloned.1.call-done = bf16[6144,2,2048]{2,0,1:T(8,128)(2,1)} async-done(((bf16[768,2,2048]{2,0,1:T(8,128)(2,1)}), bf16[6144,2,2048]{2,0,1:T(8,128)(2,1)}) %all-gather.3.cloned.1.call-update) | async-done | bytes 50331664 | tf_op jit(solution)/shard_map/all_gather | solution.py:57
  282.7 41.5 %fusion.28 = (bf16[512,2,2048]{2,0,1:T(8,128)(2,1)}, bf16[512,2,2048]{2,0,1:T(8,128)(2,1)}, bf16[512,2,2048]{2,0,1:T(8,128)(2,1)}, bf16[512,2,2048]{2,0,1:T(8,12...) fusion(bf16[6144,2,2048]{2,0,1:T(8,128)(2,1)} %all-gather.3.clo, ...), kind=kLoop, calls=%fused_computation.108 | loop fusion | bytes 100663296 | tf_op jit(solution)/shard_map/jit(_take)/gather | solution.py:59
  327.2 9.6 %while.12 = (s32[]{:T(128)}, bf16[512,2,2048]{2,0,1:T(8,128)(2,1)}, s32[2,1]{0,1:T(1,128)S(1)}, bf16[2,512,2048]{2,1,0:T(8,128)(2,1)}, s32[]{:T(128)}) while((s32[]{:T(128)}, bf16[512,2,2048]{2,0,1:T(8,128)(2,1)}, s32[2,1]{0,1:T(1,128)S(1)}, bf16[2,512,2048]{2,1,0:T(8,128)(2,1)}, s32[]{:T(128)}) %tuple.161), condition=%wide.while_cond, body=%wide.while_body.sunk | while | flops 2 | bytes 4195401 | solution.py:59
  339.9 9.5 %while.13 = (s32[]{:T(128)}, bf16[512,2,2048]{2,0,1:T(8,128)(2,1)}, s32[2,1]{0,1:T(1,128)S(1)}, bf16[2,512,2048]{2,1,0:T(8,128)(2,1)}, s32[]{:T(128)}) while((s32[]{:T(128)}, bf16[512,2,2048]{2,0,1:T(8,128)(2,1)}, s32[2,1]{0,1:T(1,128)S(1)}, bf16[2,512,2048]{2,1,0:T(8,128)(2,1)}, s32[]{:T(128)}) %tuple.205), condition=%wide.while_cond.1, body=%wide.while_body.1.sunk | while | flops 2 | bytes 4195401 | solution.py:59
  352.0 8.8 %while.14 = (s32[]{:T(128)}, bf16[512,2,2048]{2,0,1:T(8,128)(2,1)}, s32[2,1]{0,1:T(1,128)S(1)}, bf16[2,512,2048]{2,1,0:T(8,128)(2,1)}, s32[]{:T(128)}) while((s32[]{:T(128)}, bf16[512,2,2048]{2,0,1:T(8,128)(2,1)}, s32[2,1]{0,1:T(1,128)S(1)}, bf16[2,512,2048]{2,1,0:T(8,128)(2,1)}, s32[]{:T(128)}) %tuple.206), condition=%wide.while_cond.2, body=%wide.while_body.2.sunk | while | flops 2 | bytes 4195401 | solution.py:59
  363.4 9.2 %while.15 = (s32[]{:T(128)}, bf16[512,2,2048]{2,0,1:T(8,128)(2,1)}, s32[2,1]{0,1:T(1,128)S(1)}, bf16[2,512,2048]{2,1,0:T(8,128)(2,1)}, s32[]{:T(128)}) while((s32[]{:T(128)}, bf16[512,2,2048]{2,0,1:T(8,128)(2,1)}, s32[2,1]{0,1:T(1,128)S(1)}, bf16[2,512,2048]{2,1,0:T(8,128)(2,1)}, s32[]{:T(128)}) %tuple.207), condition=%wide.while_cond.3, body=%wide.while_body.3.sunk | while | flops 2 | bytes 4195401 | solution.py:59
  375.1 9.1 %while.16 = (s32[]{:T(128)}, bf16[512,2,2048]{2,0,1:T(8,128)(2,1)}, s32[2,1]{0,1:T(1,128)S(1)}, bf16[2,512,2048]{2,1,0:T(8,128)(2,1)}, s32[]{:T(128)}) while((s32[]{:T(128)}, bf16[512,2,2048]{2,0,1:T(8,128)(2,1)}, s32[2,1]{0,1:T(1,128)S(1)}, bf16[2,512,2048]{2,1,0:T(8,128)(2,1)}, s32[]{:T(128)}) %tuple.208), condition=%wide.while_cond.4, body=%wide.while_body.4.sunk | while | flops 2 | bytes 4195401 | solution.py:59
  386.7 8.8 %while.17 = (s32[]{:T(128)}, bf16[512,2,2048]{2,0,1:T(8,128)(2,1)}, s32[2,1]{0,1:T(1,128)S(1)}, bf16[2,512,2048]{2,1,0:T(8,128)(2,1)}, s32[]{:T(128)}) while((s32[]{:T(128)}, bf16[512,2,2048]{2,0,1:T(8,128)(2,1)}, s32[2,1]{0,1:T(1,128)S(1)}, bf16[2,512,2048]{2,1,0:T(8,128)(2,1)}, s32[]{:T(128)}) %tuple.209), condition=%wide.while_cond.5, body=%wide.while_body.5.sunk | while | flops 2 | bytes 4195401 | solution.py:59
  398.1 8.8 %while.18 = (s32[]{:T(128)}, bf16[512,2,2048]{2,0,1:T(8,128)(2,1)}, s32[2,1]{0,1:T(1,128)S(1)}, bf16[2,512,2048]{2,1,0:T(8,128)(2,1)}, s32[]{:T(128)}) while((s32[]{:T(128)}, bf16[512,2,2048]{2,0,1:T(8,128)(2,1)}, s32[2,1]{0,1:T(1,128)S(1)}, bf16[2,512,2048]{2,1,0:T(8,128)(2,1)}, s32[]{:T(128)}) %tuple.210), condition=%wide.while_cond.6, body=%wide.while_body.6.sunk | while | flops 2 | bytes 4195401 | solution.py:59
  409.4 9.3 %while.19 = (s32[]{:T(128)}, bf16[512,2,2048]{2,0,1:T(8,128)(2,1)}, s32[2,1]{0,1:T(1,128)S(1)}, bf16[2,512,2048]{2,1,0:T(8,128)(2,1)}, s32[]{:T(128)}) while((s32[]{:T(128)}, bf16[512,2,2048]{2,0,1:T(8,128)(2,1)}, s32[2,1]{0,1:T(1,128)S(1)}, bf16[2,512,2048]{2,1,0:T(8,128)(2,1)}, s32[]{:T(128)}) %tuple.211), condition=%wide.while_cond.7, body=%wide.while_body.7.sunk | while | flops 2 | bytes 4195401 | solution.py:59
  421.2 8.8 %while.20 = (s32[]{:T(128)}, bf16[512,2,2048]{2,0,1:T(8,128)(2,1)}, s32[2,1]{0,1:T(1,128)S(1)}, bf16[2,512,2048]{2,1,0:T(8,128)(2,1)}, s32[]{:T(128)}) while((s32[]{:T(128)}, bf16[512,2,2048]{2,0,1:T(8,128)(2,1)}, s32[2,1]{0,1:T(1,128)S(1)}, bf16[2,512,2048]{2,1,0:T(8,128)(2,1)}, s32[]{:T(128)}) %tuple.212), condition=%wide.while_cond.8, body=%wide.while_body.8.sunk | while | flops 2 | bytes 4195401 | solution.py:59
  432.5 8.7 %while.21 = (s32[]{:T(128)}, bf16[512,2,2048]{2,0,1:T(8,128)(2,1)}, s32[2,1]{0,1:T(1,128)S(1)}, bf16[2,512,2048]{2,1,0:T(8,128)(2,1)}, s32[]{:T(128)}) while((s32[]{:T(128)}, bf16[512,2,2048]{2,0,1:T(8,128)(2,1)}, s32[2,1]{0,1:T(1,128)S(1)}, bf16[2,512,2048]{2,1,0:T(8,128)(2,1)}, s32[]{:T(128)}) %tuple.213), condition=%wide.while_cond.9, body=%wide.while_body.9.sunk | while | flops 2 | bytes 4195401 | solution.py:59
  443.9 8.9 %while.22 = (s32[]{:T(128)}, bf16[512,2,2048]{2,0,1:T(8,128)(2,1)}, s32[2,1]{0,1:T(1,128)S(1)}, bf16[2,512,2048]{2,1,0:T(8,128)(2,1)}, s32[]{:T(128)}) while((s32[]{:T(128)}, bf16[512,2,2048]{2,0,1:T(8,128)(2,1)}, s32[2,1]{0,1:T(1,128)S(1)}, bf16[2,512,2048]{2,1,0:T(8,128)(2,1)}, s32[]{:T(128)}) %tuple.214), condition=%wide.while_cond.10, body=%wide.while_body.10.sunk | while | flops 2 | bytes 4195401 | solution.py:59
  455.3 9.4 %while.23 = (s32[]{:T(128)}, bf16[512,2,2048]{2,0,1:T(8,128)(2,1)}, s32[2,1]{0,1:T(1,128)S(1)}, bf16[2,512,2048]{2,1,0:T(8,128)(2,1)}, s32[]{:T(128)}) while((s32[]{:T(128)}, bf16[512,2,2048]{2,0,1:T(8,128)(2,1)}, s32[2,1]{0,1:T(1,128)S(1)}, bf16[2,512,2048]{2,1,0:T(8,128)(2,1)}, s32[]{:T(128)}) %tuple.215), condition=%wide.while_cond.11, body=%wide.while_body.11.sunk | while | flops 2 | bytes 4195401 | solution.py:59
  510.1 25.9 %fusion.1 = f32[2,6144,128]{1,2,0:T(8,128)} fusion(bf16[2,128,2048]{2,1,0:T(8,128)(2,1)S(1)} %bitcast.149, bf16[6144,2,2048]{2,0,1:T(8,128)(2,1)} %bitcast_dynamic-update-slice_fusion.12, pred[2]{0:T(512)(128)(4,1)S(1)} %maximum_compare_fusion), kind=kOutput, calls=%fused_computation.33 | convolution fusion | flops 6467616768 | bytes 57671680 | tf_op jit(solution)/shard_map/bri,dbi->brd/dot_general | solution.py:60
  536.0 10.6 %gather_fusion = f32[256,6144]{1,0:T(8,128)} fusion(f32[256,6144]{1,0:T(8,128)} %bitcast.147, s32[1024]{0:T(1024)S(1)} %copy-done.14), kind=kCustom, calls=%fused_computation | custom fusion | bytes 12583936 | tf_op jit(solution)/shard_map/gather | solution.py:66
  546.6 8.4 %reshape.505 = f32[128,2,6144]{2,1,0:T(2,128)} reshape(f32[256,6144]{1,0:T(8,128)} %gather_fusion) | data formatting | bytes 12582912 | tf_op jit(solution)/shard_map/gather | solution.py:66
  555.0 20.2 %fusion = f32[2,128,2048]{2,1,0:T(8,128)} fusion(bf16[6144,2,2048]{2,0,1:T(8,128)(2,1)} %bitcast_dynamic-update-slice_fusion.12, pred[2]{0:T(512)(128)(4,1)S(1)} %maximum_compare_fusion, bf16[2,128,6144]{2,1,0:T(8,128)(2,1)S(1)} %bitcast.148, pred[2,128]{1,0:T(4,128)(4,1)S(1)} %copy-done.22), kind=kOutput, calls=%fused_computation.32 | convolution fusion | flops 6469189632 | bytes 55574784 | tf_op jit(solution)/shard_map/brd,dbi->bri/dot_general | solution.py:63
  581.0 11.9 %multiply_reduce_fusion = bf16[128,6144]{1,0:T(8,128)(2,1)} fusion(f32[128,2,6144]{2,1,0:T(2,128)} %reshape.505, f32[128,2]{1,0:T(8,128)S(1)} %copy.20), kind=kLoop, calls=%fused_computation.35 | loop fusion | flops 2359296 | bytes 7865344 | tf_op jit(solution)/shard_map/reduce_sum | solution.py:66
  592.9 12.6 %copy.30 = bf16[768,2,2048]{2,1,0:T(2,128)(2,1)} copy(bf16[768,2,2048]{2,0,1:T(8,128)(2,1)} %reduce-scatter.5.cloned.1.call-done) | data formatting | bytes 12582912
  605.5 12.9 %psum.7 = f32[128,2]{0,1:T(2,128)} all-reduce(f32[128,2]{0,1:T(2,128)S(1)} %get-tuple-element.225), channel_id=1, replica_groups=mesh['fsdp'=8,'ep'=4] {'ep'}, use_global_device_ids=true, to_apply=%region_14.15 | all-reduce | flops 256 | bytes 2048 | tf_op jit(solution)/shard_map/psum | solution.py:82
  618.5 10.2 %reduce-scatter.3.cloned.1.call-done = bf16[128,1536]{1,0:T(8,128)(2,1)} async-done(((bf16[128,6144]{1,0:T(8,128)(2,1)}), bf16[128,1536]{1,0:T(8,128)(2,1)}) %reduce-scatter.3.cloned.1.call-update) | async-done | bytes 393232 | tf_op jit(solution)/shard_map/reduce_scatter | solution.py:77
  (170 shorter events, 216.5 us)
Async XLA Ops:
  7.2 42.2 %all-gather.5.cloned.1.call-start = ((), (), s32[]{:S(2)}) async-start(), calls=%async_computation.4 | async-start | bytes 1966080 | tf_op jit(solution)/shard_map/all_gather | solution.py:46
  7.9 274.8 %all-gather.3.cloned.1.call-start = ((), (), s32[]{:S(2)}) async-start(), calls=%async_computation.2 | async-start | bytes 56623104 | tf_op jit(solution)/shard_map/all_gather | solution.py:57
  16.3 4.7 copy-start.19
  16.4 576.5 %reduce-scatter.5.cloned.1.call-start = ((), (), s32[]{:S(2)}) async-start(), calls=%async_computation.5 | async-start | bytes 56623104 | tf_op jit(solution)/shard_map/reduce_scatter | solution.py:69
  17.1 6.4 %copy-start.17 = (s32[128,2]{0,1:T(2,128)}, s32[128,2]{0,1:T(2,128)S(1)}, u32[]{:S(2)}) copy-start(s32[128,2]{0,1:T(2,128)S(1)} %get-tuple-element.112) | copy-start | bytes 3076
  23.2 33.3 %copy-start.15 = (f32[256]{0:T(256)}, f32[256]{0:T(256)S(1)}, u32[]{:S(2)}) copy-start(f32[256]{0:T(256)S(1)} %scatter_custom_fusion) | copy-start | bytes 3076
  56.5 25.0 %copy-start.11 = (bf16[256,6144]{1,0:T(8,128)(2,1)}, bf16[256,6144]{1,0:T(8,128)(2,1)S(1)}, u32[]{:S(2)}) copy-start(bf16[256,6144]{1,0:T(8,128)(2,1)S(1)} %gather_fusion.1) | copy-start | bytes 9437188
  81.5 547.2 %reduce-scatter.3.cloned.1.call-start = ((), (), s32[]{:S(2)}) async-start(), calls=%async_computation.3 | async-start | bytes 1966080 | tf_op jit(solution)/shard_map/reduce_scatter | solution.py:77
  464.7 5.3 copy-start.1
  470.0 3.8 copy-start.2
  473.9 3.9 copy-start.3
  477.7 3.9 copy-start.4
  481.6 3.7 copy-start.5
  485.3 3.7 copy-start.6
  489.0 3.7 copy-start.7
  492.8 3.7 copy-start.8
  496.5 3.7 copy-start.9
  500.2 4.0 copy-start.10
  504.2 3.7 copy-start
  510.1 25.9 %copy-start.14 = (s32[1024]{0:T(1024)S(1)}, s32[1024]{0:T(1024)}, u32[]{:S(2)}) copy-start(s32[1024]{0:T(1024)} %pad_clamp_fusion.1) | copy-start | bytes 12292
  546.6 8.4 %copy-start.12 = (bf16[256,6144]{1,0:T(8,128)(2,1)S(1)}, bf16[256,6144]{1,0:T(8,128)(2,1)}, u32[]{:S(2)}) copy-start(bf16[256,6144]{1,0:T(8,128)(2,1)} %copy-done.11) | copy-start | bytes 9437188
  546.6 8.4 %copy-start.22 = (pred[2,128]{1,0:T(4,128)(4,1)S(1)}, pred[2,128]{1,0:T(4,128)(4,1)}, u32[]{:S(2)}) copy-start(pred[2,128]{1,0:T(4,128)(4,1)} %fusion.30) | copy-start | bytes 772
  555.0 20.2 %copy-start.16 = (f32[256]{0:T(256)S(1)}, f32[256]{0:T(256)}, u32[]{:S(2)}) copy-start(f32[256]{0:T(256)} %copy-done.15) | copy-start | bytes 3076
  578.4 2.4 copy-start.20
  (3 other events, 5.3 us)
Sparse Core Ops, SparseCore 0:
  9.6 39.7 all-gather.4
  51.9 230.7 all-gather.2
  286.3 285.8 reduce-scatter.4
  593.0 35.6 reduce-scatter.2
where the time goes:
time: 642 us; the launch traced here: 635 us
  local copies, waits for them, and re-layouts  283 us (44%)
  waiting for transfers between devices  236 us (37%)
  matrix products  71.1 us (11%)
  other arithmetic  17 us (3%)
  between operations  14.3 us (2%)
  blocking collectives  12.9 us (2%)
    all_gather x1, waiting for transfers between devices, local(): piece = lax.all_gather(w_down, 'fsdp', axis=0, tiled=True)  200 us
    gather x48, local copies, waits for them, and re-layouts  109 us
    unnamed x73, local copies, waits for them, and re-layouts  98.7 us
    gather x1, local copies, waits for them, and re-layouts, local(): chosen = jnp.take(piece, safe_exp, axis=1)  41.5 us
    dot_general x1, matrix products, local(): jnp.einsum('bri,dbi->brd', hid_blocks, chosen, preferred_element_type=jnp...  25.9 us
    all_gather x1, waiting for transfers between devices, local(): full_grads = lax.all_gather(grad_out, 'ep', axis=1, tiled=True)  25.9 us
    dot_general x1, matrix products, local(): jnp.einsum('rd,rei->dei', scaled, masked_hid, preferred_element_type=jnp....  24.9 us
    dot_general x1, matrix products, local(): jnp.einsum('brd,dbi->bri', routed_blocks, chosen, preferred_element_type=...  20.2 us
  transfers between devices with their start and end apart: 4, of which 3 were waited for; matrix products, arithmetic and copies ran while one was open for 56% of the time, Pallas kernels for 0%

commit v1 on v0

--- a/solution.py
+++ b/solution.py
@@ -43,7 +43,12 @@
     )
     safe_exp = jnp.maximum(block_exp, 0)
     prob_valid = probs * valid.astype(jnp.float32)
-    full_grads = lax.all_gather(grad_out, "ep", axis=1, tiled=True)
+    ring = [grad_out]
+    for hop in range(3):
+        ring.append(lax.ppermute(ring[-1], "ep", [(dev, (dev + 1) % 4) for dev in range(4)]))
+    full_grads = jnp.roll(
+        jnp.concatenate(ring[::-1], axis=1), (lax.axis_index("ep") + 1) * ring[0].shape[1], axis=1
+    )
     model_width = full_grads.shape[1]
     routed = jnp.where(row_live[:, None] > 0, full_grads[row_tok], jnp.zeros((), jnp.bfloat16))
     scaled = (row_prob[:, None] * routed.astype(jnp.float32)).astype(jnp.bfloat16)

time: 642 us -> 612 us (0.953)
  waiting for transfers between devices: 236 us -> 206 us
    all_gather x1, waiting for transfers between devices: 200 us -> 167 us  [local(): piece = lax.all_gather(w_down, 'fsdp', axis=0, tiled=True)]
    ppermute x0 -> x3, waiting for transfers between devices: none -> 28.4 us  [local(): lax.ppermute(ring[-1], 'ep', [(dev, (dev + 1) % 4) for dev in range(4)])]
    all_gather x1 -> x0, waiting for transfers between devices: 25.9 us -> none  [local(): full_grads = lax.all_gather(grad_out, 'ep', axis=1, tiled=True)]
    unnamed x73 -> x80, local copies, waits for them, and re-layouts: 98.7 us -> 101 us
  transfers between devices with their start and end apart: 4 -> 6, of which waited for: 3 -> 5; matrix products, arithmetic and copies ran while one was open for 56% -> 57% of each run, Pallas kernels for 0% -> 0%
where the time goes in v1:
time: 612 us; the launch traced here: 605 us
  local copies, waits for them, and re-layouts  282 us (46%)
  waiting for transfers between devices  206 us (34%)
  matrix products  69.4 us (11%)
  other arithmetic  16.5 us (3%)
  between operations  14.4 us (2%)
  blocking collectives  12.8 us (2%)
    all_gather x1, waiting for transfers between devices, local(): piece = lax.all_gather(w_down, 'fsdp', axis=0, tiled=True)  167 us
    gather x48, local copies, waits for them, and re-layouts  109 us
    unnamed x80, local copies, waits for them, and re-layouts  101 us
    gather x1, local copies, waits for them, and re-layouts, local(): chosen = jnp.take(piece, safe_exp, axis=1)  41.5 us
    ppermute x3, waiting for transfers between devices, local(): lax.ppermute(ring[-1], 'ep', [(dev, (dev + 1) % 4) for dev in range(4)])  28.4 us
    dot_general x1, matrix products, local(): jnp.einsum('bri,dbi->brd', hid_blocks, chosen, preferred_element_type=jnp...  25.5 us
    dot_general x1, matrix products, local(): jnp.einsum('rd,rei->dei', scaled, masked_hid, preferred_element_type=jnp....  22.6 us
    dot_general x1, matrix products, local(): jnp.einsum('brd,dbi->bri', routed_blocks, chosen, preferred_element_type=...  21.3 us
  transfers between devices with their start and end apart: 6, of which 5 were waited for; matrix products, arithmetic and copies ran while one was open for 57% of the time, Pallas kernels for 0%

profile of v1, /device:TPU:0, one launch (start us, length us, event | category | flops | bytes accessed | tf_op | source)
XLA Modules:
  0.0 605.2 jit_solution(6639048210511241270)
XLA Ops:
  30.8 12.0 %collective-permute-done.1 = bf16[128,1536]{1,0:T(8,128)(2,1)S(1)} collective-permute-done((bf16[128,1536]{1,0:T(8,128)(2,1)S(1)}, bf16[128,1536]{1,0:T(8,128)(2,1)S(1)}, u32[]{:S(2)}, u32[]{:S(2)}) %collective-permute-start.1) | collective-permute-done | bytes 393248 | tf_op jit(solution)/shard_map/ppermute | solution.py:48
  43.4 11.1 %collective-permute-done.2 = bf16[128,1536]{1,0:T(8,128)(2,1)S(1)} collective-permute-done((bf16[128,1536]{1,0:T(8,128)(2,1)S(1)}, bf16[128,1536]{1,0:T(8,128)(2,1)S(1)}, u32[]{:S(2)}, u32[]{:S(2)}) %collective-permute-start.2) | collective-permute-done | bytes 393248 | tf_op jit(solution)/shard_map/ppermute | solution.py:48
  59.6 22.6 %convolution_convert_fusion = bf16[6144,2,2048]{2,0,1:T(8,128)(2,1)} fusion(bf16[256,6144]{1,0:T(8,128)(2,1)} %gather_fusion.1, f32[256]{0:T(256)S(1)} %scatter_custom_fusion, pred[256]{0:T(512)(128)(4,1)S(1)} %broadcast_compare_fusion, bf16[256,2]{0,1:T(2,128)(2,1)S(1)} %compare_convert_fusion, bf16[256,2048]{1,0:T(8,128)(2,1)S(1)} %copy-done.12), kind=kOutput, calls=%fused_computation.31 | convolution fusion | flops 12920553472 | bytes 54528256 | tf_op jit(solution)/shard_map/rd,rei->dei/dot_general | solution.py:75
  83.3 167.0 %all-gather.2.cloned.1.call-done = bf16[6144,2,2048]{2,0,1:T(8,128)(2,1)} async-done(((bf16[768,2,2048]{2,0,1:T(8,128)(2,1)}), bf16[6144,2,2048]{2,0,1:T(8,128)(2,1)}) %all-gather.2.cloned.1.call-update) | async-done | bytes 50331664 | tf_op jit(solution)/shard_map/all_gather | solution.py:62
  250.3 41.5 %fusion.28 = (bf16[512,2,2048]{2,0,1:T(8,128)(2,1)}, bf16[512,2,2048]{2,0,1:T(8,128)(2,1)}, bf16[512,2,2048]{2,0,1:T(8,128)(2,1)}, bf16[512,2,2048]{2,0,1:T(8,12...) fusion(bf16[6144,2,2048]{2,0,1:T(8,128)(2,1)} %all-gather.2.clo, ...), kind=kLoop, calls=%fused_computation.117 | loop fusion | bytes 100663296 | tf_op jit(solution)/shard_map/jit(_take)/gather | solution.py:64
  294.9 9.6 %while.12 = (s32[]{:T(128)}, bf16[512,2,2048]{2,0,1:T(8,128)(2,1)}, s32[2,1]{0,1:T(1,128)S(1)}, bf16[2,512,2048]{2,1,0:T(8,128)(2,1)}, s32[]{:T(128)}) while((s32[]{:T(128)}, bf16[512,2,2048]{2,0,1:T(8,128)(2,1)}, s32[2,1]{0,1:T(1,128)S(1)}, bf16[2,512,2048]{2,1,0:T(8,128)(2,1)}, s32[]{:T(128)}) %tuple.161), condition=%wide.while_cond, body=%wide.while_body.sunk | while | flops 2 | bytes 4195401 | solution.py:64
  307.6 9.4 %while.13 = (s32[]{:T(128)}, bf16[512,2,2048]{2,0,1:T(8,128)(2,1)}, s32[2,1]{0,1:T(1,128)S(1)}, bf16[2,512,2048]{2,1,0:T(8,128)(2,1)}, s32[]{:T(128)}) while((s32[]{:T(128)}, bf16[512,2,2048]{2,0,1:T(8,128)(2,1)}, s32[2,1]{0,1:T(1,128)S(1)}, bf16[2,512,2048]{2,1,0:T(8,128)(2,1)}, s32[]{:T(128)}) %tuple.203), condition=%wide.while_cond.1, body=%wide.while_body.1.sunk | while | flops 2 | bytes 4195401 | solution.py:64
  319.6 8.8 %while.14 = (s32[]{:T(128)}, bf16[512,2,2048]{2,0,1:T(8,128)(2,1)}, s32[2,1]{0,1:T(1,128)S(1)}, bf16[2,512,2048]{2,1,0:T(8,128)(2,1)}, s32[]{:T(128)}) while((s32[]{:T(128)}, bf16[512,2,2048]{2,0,1:T(8,128)(2,1)}, s32[2,1]{0,1:T(1,128)S(1)}, bf16[2,512,2048]{2,1,0:T(8,128)(2,1)}, s32[]{:T(128)}) %tuple.204), condition=%wide.while_cond.2, body=%wide.while_body.2.sunk | while | flops 2 | bytes 4195401 | solution.py:64
  331.0 9.2 %while.15 = (s32[]{:T(128)}, bf16[512,2,2048]{2,0,1:T(8,128)(2,1)}, s32[2,1]{0,1:T(1,128)S(1)}, bf16[2,512,2048]{2,1,0:T(8,128)(2,1)}, s32[]{:T(128)}) while((s32[]{:T(128)}, bf16[512,2,2048]{2,0,1:T(8,128)(2,1)}, s32[2,1]{0,1:T(1,128)S(1)}, bf16[2,512,2048]{2,1,0:T(8,128)(2,1)}, s32[]{:T(128)}) %tuple.205), condition=%wide.while_cond.3, body=%wide.while_body.3.sunk | while | flops 2 | bytes 4195401 | solution.py:64
  342.8 9.1 %while.16 = (s32[]{:T(128)}, bf16[512,2,2048]{2,0,1:T(8,128)(2,1)}, s32[2,1]{0,1:T(1,128)S(1)}, bf16[2,512,2048]{2,1,0:T(8,128)(2,1)}, s32[]{:T(128)}) while((s32[]{:T(128)}, bf16[512,2,2048]{2,0,1:T(8,128)(2,1)}, s32[2,1]{0,1:T(1,128)S(1)}, bf16[2,512,2048]{2,1,0:T(8,128)(2,1)}, s32[]{:T(128)}) %tuple.206), condition=%wide.while_cond.4, body=%wide.while_body.4.sunk | while | flops 2 | bytes 4195401 | solution.py:64
  354.3 8.8 %while.17 = (s32[]{:T(128)}, bf16[512,2,2048]{2,0,1:T(8,128)(2,1)}, s32[2,1]{0,1:T(1,128)S(1)}, bf16[2,512,2048]{2,1,0:T(8,128)(2,1)}, s32[]{:T(128)}) while((s32[]{:T(128)}, bf16[512,2,2048]{2,0,1:T(8,128)(2,1)}, s32[2,1]{0,1:T(1,128)S(1)}, bf16[2,512,2048]{2,1,0:T(8,128)(2,1)}, s32[]{:T(128)}) %tuple.207), condition=%wide.while_cond.5, body=%wide.while_body.5.sunk | while | flops 2 | bytes 4195401 | solution.py:64
  365.7 8.8 %while.18 = (s32[]{:T(128)}, bf16[512,2,2048]{2,0,1:T(8,128)(2,1)}, s32[2,1]{0,1:T(1,128)S(1)}, bf16[2,512,2048]{2,1,0:T(8,128)(2,1)}, s32[]{:T(128)}) while((s32[]{:T(128)}, bf16[512,2,2048]{2,0,1:T(8,128)(2,1)}, s32[2,1]{0,1:T(1,128)S(1)}, bf16[2,512,2048]{2,1,0:T(8,128)(2,1)}, s32[]{:T(128)}) %tuple.208), condition=%wide.while_cond.6, body=%wide.while_body.6.sunk | while | flops 2 | bytes 4195401 | solution.py:64
  377.1 9.3 %while.19 = (s32[]{:T(128)}, bf16[512,2,2048]{2,0,1:T(8,128)(2,1)}, s32[2,1]{0,1:T(1,128)S(1)}, bf16[2,512,2048]{2,1,0:T(8,128)(2,1)}, s32[]{:T(128)}) while((s32[]{:T(128)}, bf16[512,2,2048]{2,0,1:T(8,128)(2,1)}, s32[2,1]{0,1:T(1,128)S(1)}, bf16[2,512,2048]{2,1,0:T(8,128)(2,1)}, s32[]{:T(128)}) %tuple.209), condition=%wide.while_cond.7, body=%wide.while_body.7.sunk | while | flops 2 | bytes 4195401 | solution.py:64
  388.9 8.8 %while.20 = (s32[]{:T(128)}, bf16[512,2,2048]{2,0,1:T(8,128)(2,1)}, s32[2,1]{0,1:T(1,128)S(1)}, bf16[2,512,2048]{2,1,0:T(8,128)(2,1)}, s32[]{:T(128)}) while((s32[]{:T(128)}, bf16[512,2,2048]{2,0,1:T(8,128)(2,1)}, s32[2,1]{0,1:T(1,128)S(1)}, bf16[2,512,2048]{2,1,0:T(8,128)(2,1)}, s32[]{:T(128)}) %tuple.210), condition=%wide.while_cond.8, body=%wide.while_body.8.sunk | while | flops 2 | bytes 4195401 | solution.py:64
  400.2 8.7 %while.21 = (s32[]{:T(128)}, bf16[512,2,2048]{2,0,1:T(8,128)(2,1)}, s32[2,1]{0,1:T(1,128)S(1)}, bf16[2,512,2048]{2,1,0:T(8,128)(2,1)}, s32[]{:T(128)}) while((s32[]{:T(128)}, bf16[512,2,2048]{2,0,1:T(8,128)(2,1)}, s32[2,1]{0,1:T(1,128)S(1)}, bf16[2,512,2048]{2,1,0:T(8,128)(2,1)}, s32[]{:T(128)}) %tuple.211), condition=%wide.while_cond.9, body=%wide.while_body.9.sunk | while | flops 2 | bytes 4195401 | solution.py:64
  411.5 8.9 %while.22 = (s32[]{:T(128)}, bf16[512,2,2048]{2,0,1:T(8,128)(2,1)}, s32[2,1]{0,1:T(1,128)S(1)}, bf16[2,512,2048]{2,1,0:T(8,128)(2,1)}, s32[]{:T(128)}) while((s32[]{:T(128)}, bf16[512,2,2048]{2,0,1:T(8,128)(2,1)}, s32[2,1]{0,1:T(1,128)S(1)}, bf16[2,512,2048]{2,1,0:T(8,128)(2,1)}, s32[]{:T(128)}) %tuple.212), condition=%wide.while_cond.10, body=%wide.while_body.10.sunk | while | flops 2 | bytes 4195401 | solution.py:64
  423.0 9.4 %while.23 = (s32[]{:T(128)}, bf16[512,2,2048]{2,0,1:T(8,128)(2,1)}, s32[2,1]{0,1:T(1,128)S(1)}, bf16[2,512,2048]{2,1,0:T(8,128)(2,1)}, s32[]{:T(128)}) while((s32[]{:T(128)}, bf16[512,2,2048]{2,0,1:T(8,128)(2,1)}, s32[2,1]{0,1:T(1,128)S(1)}, bf16[2,512,2048]{2,1,0:T(8,128)(2,1)}, s32[]{:T(128)}) %tuple.213), condition=%wide.while_cond.11, body=%wide.while_body.11.sunk | while | flops 2 | bytes 4195401 | solution.py:64
  479.0 21.3 %fusion = f32[2,128,2048]{2,1,0:T(8,128)} fusion(bf16[6144,2,2048]{2,0,1:T(8,128)(2,1)} %bitcast_dynamic-update-slice_fusion.12, pred[2]{0:T(512)(128)(4,1)S(1)} %maximum_compare_fusion, bf16[2,128,6144]{2,1,0:T(8,128)(2,1)S(1)} %bitcast.148, pred[2,128]{1,0:T(4,128)(4,1)S(1)} %fusion.30), kind=kOutput, calls=%fused_computation.32 | convolution fusion | flops 6469189632 | bytes 55574784 | tf_op jit(solution)/shard_map/brd,dbi->bri/dot_general | solution.py:68
  505.9 25.5 %fusion.1 = f32[2,6144,128]{1,2,0:T(8,128)} fusion(bf16[2,128,2048]{2,1,0:T(8,128)(2,1)S(1)} %bitcast.149, bf16[6144,2,2048]{2,0,1:T(8,128)(2,1)} %bitcast_dynamic-update-slice_fusion.12, pred[2]{0:T(512)(128)(4,1)S(1)} %maximum_compare_fusion), kind=kOutput, calls=%fused_computation.33 | convolution fusion | flops 6467616768 | bytes 57671680 | tf_op jit(solution)/shard_map/bri,dbi->brd/dot_general | solution.py:65
  531.4 10.6 %gather_fusion = f32[256,6144]{1,0:T(8,128)} fusion(f32[256,6144]{1,0:T(8,128)} %bitcast.147, s32[1024]{0:T(1024)S(1)} %copy-done.14), kind=kCustom, calls=%fused_computation | custom fusion | bytes 12583936 | tf_op jit(solution)/shard_map/gather | solution.py:71
  550.4 11.9 %multiply_reduce_fusion = bf16[128,6144]{1,0:T(8,128)(2,1)} fusion(f32[128,2,6144]{2,1,0:T(2,128)} %reshape.505, f32[128,2]{1,0:T(8,128)S(1)} %copy.20), kind=kLoop, calls=%fused_computation.35 | loop fusion | flops 2359296 | bytes 7865344 | tf_op jit(solution)/shard_map/reduce_sum | solution.py:71
  562.3 12.6 %copy.30 = bf16[768,2,2048]{2,1,0:T(2,128)(2,1)} copy(bf16[768,2,2048]{2,0,1:T(8,128)(2,1)} %reduce-scatter.5.cloned.1.call-done) | data formatting | bytes 12582912
  574.9 12.8 %psum.7 = f32[128,2]{0,1:T(2,128)} all-reduce(f32[128,2]{0,1:T(2,128)S(1)} %get-tuple-element.225), channel_id=1, replica_groups=mesh['fsdp'=8,'ep'=4] {'ep'}, use_global_device_ids=true, to_apply=%region_14.15 | all-reduce | flops 256 | bytes 2048 | tf_op jit(solution)/shard_map/psum | solution.py:87
  587.7 10.6 %reduce-scatter.3.cloned.1.call-done = bf16[128,1536]{1,0:T(8,128)(2,1)} async-done(((bf16[128,6144]{1,0:T(8,128)(2,1)}), bf16[128,1536]{1,0:T(8,128)(2,1)}) %reduce-scatter.3.cloned.1.call-update) | async-done | bytes 393232 | tf_op jit(solution)/shard_map/reduce_scatter | solution.py:82
  (182 shorter events, 231.1 us)
Async XLA Ops:
  7.2 243.2 %all-gather.2.cloned.1.call-start = ((), (), s32[]{:S(2)}) async-start(), calls=%async_computation.2 | async-start | bytes 56623104 | tf_op jit(solution)/shard_map/all_gather | solution.py:62
  15.6 4.0 copy-start.22
  15.6 8.0 %copy-start.20 = (f32[128,2]{0,1:T(2,128)S(1)}, f32[128,2]{0,1:T(2,128)}, u32[]{:S(2)}) copy-start(f32[128,2]{0,1:T(2,128)} %param.8) | copy-start | bytes 3076
  15.6 546.7 %reduce-scatter.5.cloned.1.call-start = ((), (), s32[]{:S(2)}) async-start(), calls=%async_computation.4 | async-start | bytes 56623104 | tf_op jit(solution)/shard_map/reduce_scatter | solution.py:74
  16.6 14.2 %collective-permute-start = (bf16[128,1536]{1,0:T(8,128)(2,1)S(1)}, bf16[128,1536]{1,0:T(8,128)(2,1)S(1)}, u32[]{:S(2)}, u32[]{:S(2)}) collective-permute-start(bf16[128,1536]{1,0:T(8,128)(2,1)S(1)} %copy-done.15), channel_id=1, source_target_pairs={{0,1},{1,2},{2,3},{3,0},{4,5},{5,6},{6,7},{7,4},{8,9},{9,10},{10,1... | collective-permute-start | bytes 1179656 | tf_op jit(solution)/shard_map/ppermute | solution.py:48
  19.7 35.1 %copy-start.18 = (s32[128,2]{0,1:T(2,128)}, s32[128,2]{0,1:T(2,128)S(1)}, u32[]{:S(2)}) copy-start(s32[128,2]{0,1:T(2,128)S(1)} %get-tuple-element.112) | copy-start | bytes 3076
  25.3 34.3 %copy-start.16 = (f32[256]{0:T(256)}, f32[256]{0:T(256)S(1)}, u32[]{:S(2)}) copy-start(f32[256]{0:T(256)S(1)} %scatter_custom_fusion) | copy-start | bytes 3076
  30.8 12.1 %collective-permute-start.1 = (bf16[128,1536]{1,0:T(8,128)(2,1)S(1)}, bf16[128,1536]{1,0:T(8,128)(2,1)S(1)}, u32[]{:S(2)}, u32[]{:S(2)}) collective-permute-start(bf16[128,1536]{1,0:T(8,128)(2,1)S(1)} %collective-permute-done), channel_id=1, source_target_pairs={{0,1},{1,2},{2,3},{3,0},{4,5},{5,6},{6,7},{7,4},{8,9},{9,10},{10,1... | collective-permute-start | bytes 1179656 | tf_op jit(solution)/shard_map/ppermute | solution.py:48
  42.9 11.7 %collective-permute-start.2 = (bf16[128,1536]{1,0:T(8,128)(2,1)S(1)}, bf16[128,1536]{1,0:T(8,128)(2,1)S(1)}, u32[]{:S(2)}, u32[]{:S(2)}) collective-permute-start(bf16[128,1536]{1,0:T(8,128)(2,1)S(1)} %collective-permute-done.1), channel_id=1, source_target_pairs={{0,1},{1,2},{2,3},{3,0},{4,5},{5,6},{6,7},{7,4},{8,9},{9,10},{10,1... | collective-permute-start | bytes 1179656 | tf_op jit(solution)/shard_map/ppermute | solution.py:48
  55.4 4.2 copy-start.12
  82.2 516.2 %reduce-scatter.3.cloned.1.call-start = ((), (), s32[]{:S(2)}) async-start(), calls=%async_computation.3 | async-start | bytes 1966080 | tf_op jit(solution)/shard_map/reduce_scatter | solution.py:82
  432.4 5.3 copy-start.1
  437.6 3.8 copy-start.2
  441.5 3.9 copy-start.3
  445.4 3.8 copy-start.4
  449.2 3.7 copy-start.5
  452.9 3.7 copy-start.6
  456.7 3.7 copy-start.7
  460.4 3.8 copy-start.8
  464.1 3.7 copy-start.9
  467.8 4.0 copy-start.10
  471.8 3.7 copy-start
  475.5 3.5 copy-start.11
  479.0 21.3 %copy-start.17 = (f32[256]{0:T(256)S(1)}, f32[256]{0:T(256)}, u32[]{:S(2)}) copy-start(f32[256]{0:T(256)} %copy-done.16) | copy-start | bytes 3076
  (5 other events, 10.9 us)
Sparse Core Ops, SparseCore 0:
  15.7 234.5 all-gather.1
  254.0 285.8 reduce-scatter.4
  562.4 35.9 reduce-scatter.2
